TPU v7x, 256 devices: a whole 4x4x8 slice. The times are simulated.
256 devices in a mesh: ns: 64 (over z_lo, y, x), ew: 4 (over z_hi, core).
Axes of the slice: x: 4, y: 4, z: 8 (z_hi: 2, z_lo: 4; z = z_hi * 4 + z_lo), core: 2. Of those that a mesh axis runs over, the one named last changes fastest.
Arguments:
- tokens: bfloat16 [512, 512, 512], P('ns', 'ew'), may hold values from -6 to 6
- conv_gain: float32 [512], replicated, may hold values from 0.1 to 1.9
- w_expand: bfloat16 [512, 2048], replicated, may hold values from -0.25 to 0.25
- dw_kernel: float32 [3, 3, 2048], replicated, may hold values from -2 to 2
- w_project: bfloat16 [2048, 512], replicated, may hold values from -0.375 to 0.375
- block_gain: float32 [512], replicated, may hold values from 0.1 to 1.9
- block_qkv: bfloat16 [512, 1536], replicated, may hold values from -2 to 2
- block_out: bfloat16 [512, 512], replicated, may hold values from -0.25 to 0.25
- grid_gain: float32 [512], replicated, may hold values from 0.1 to 1.9
- grid_qkv: bfloat16 [512, 1536], replicated, may hold values from -2 to 2
- grid_out: bfloat16 [512, 512], replicated, may hold values from -0.25 to 0.25
Outputs:
- block_output: bfloat16 [512, 512, 512], P('ns', 'ew')
All inputs are finite; a program needn't handle non-finite values.
Results may differ from a plain program's by a relative error of at most 0.017.
Values may be sent and summed in bfloat16 or wider, within the bound.
A program may use at most 128 MiB of HBM per device.

v0:
```python
import jax
import jax.numpy as jnp
from jax import lax
from jax.sharding import PartitionSpec as P

HEADS = 16
WINDOW = 8


def with_halo(block, sides, width):
    for axis, dim in sides:
        count = lax.axis_size(axis)
        forward = [(i, i + 1) for i in range(count - 1)]
        backward = [(target, source) for source, target in forward]
        low = lax.ppermute(
            lax.slice_in_dim(block, block.shape[dim] - width, None, axis=dim), axis, forward
        )
        high = lax.ppermute(lax.slice_in_dim(block, 0, width, axis=dim), axis, backward)
        block = jnp.concatenate([low, block, high], axis=dim)
    return block


def in_blocks(x, dim, peers):
    dims = x.shape
    tiles = x.reshape(*dims[:dim], peers, dims[dim] // peers, *dims[dim + 1 :])
    return jnp.moveaxis(tiles, dim, 0)


def in_order(tiles, dim):
    tiles = jnp.moveaxis(tiles, 0, dim)
    dims = tiles.shape
    return tiles.reshape(*dims[:dim], dims[dim] * dims[dim + 1], *dims[dim + 2 :])


def joined_exchange(x, axis, axes, splits, concats):
    sizes = [lax.axis_size(a) for a in axes]
    tiles = in_blocks(x, splits[0], sizes[0])
    tiles = jnp.moveaxis(in_blocks(tiles, splits[1] + 1, sizes[1]), 0, 1)
    inside = tiles.shape[2:]
    tiles = tiles.reshape(-1, *inside)
    tiles = lax.all_to_all(tiles, axis, split_axis=0, concat_axis=0, tiled=True)
    tiles = in_order(tiles.reshape(*sizes, *inside), concats[0] + 1)
    return in_order(tiles, concats[1])


def normalize(tokens, scale_gain):
    floats = tokens.astype(jnp.float32)
    center = floats - jnp.mean(floats, axis=-1, keepdims=True)
    spread = jnp.mean(center * center, axis=-1, keepdims=True)
    return (center * lax.rsqrt(spread + 1e-05) * scale_gain).astype(jnp.bfloat16)


def expand_rows(tokens, scale_gain, w_expand):
    normed = normalize(tokens, scale_gain)
    flat_tokens = normed.reshape(-1, normed.shape[-1])
    hidden = jax.nn.gelu(jnp.dot(flat_tokens, w_expand, preferred_element_type=jnp.float32))
    return hidden.astype(jnp.bfloat16).reshape(tokens.shape[:-1] + (w_expand.shape[1],))


def depthwise(padded, dw_kernel, tile_rows, tile_cols):
    summed = jnp.zeros((tile_rows, tile_cols, padded.shape[-1]), jnp.float32)
    for offset_row in range(3):
        for offset_col in range(3):
            summed = (
                summed
                + padded[
                    offset_row : offset_row + tile_rows, offset_col : offset_col + tile_cols
                ].astype(jnp.float32)
                * dw_kernel[offset_row, offset_col]
            )
    return jax.nn.gelu(summed).astype(jnp.bfloat16)


def attend(tokens, scale_gain, w_qkv, w_out):
    layout = tokens.shape
    dim_p, dim_w, dim_q, dim_s, channels = layout
    head_dim = channels // HEADS
    normed = normalize(tokens, scale_gain).reshape(-1, channels)
    packed = jnp.dot(normed, w_qkv, preferred_element_type=jnp.float32).astype(jnp.bfloat16)
    packed = packed.reshape(dim_p, dim_w, dim_q, dim_s, 3, HEADS, head_dim)
    moved = jnp.transpose(packed, (4, 1, 3, 5, 0, 2, 6)).reshape(
        3, dim_w * dim_s, HEADS, dim_p * dim_q, head_dim
    )
    queries = moved[0]
    key_rows = moved[1]
    value_rows = moved[2]
    scores = jnp.einsum(
        "nhqd,nhkd->nhqk", queries, key_rows, preferred_element_type=jnp.float32
    ) * head_dim ** (-0.5)
    weights = jax.nn.softmax(scores, axis=-1).astype(jnp.bfloat16)
    blended = jnp.einsum(
        "nhqk,nhkd->nhqd", weights, value_rows, preferred_element_type=jnp.float32
    ).astype(jnp.bfloat16)
    blended = blended.reshape(dim_w, dim_s, HEADS, dim_p, dim_q, head_dim)
    blended = jnp.transpose(blended, (3, 0, 4, 1, 2, 5)).reshape(-1, channels)
    result = tokens.astype(jnp.float32).reshape(-1, channels) + jnp.dot(
        blended, w_out, preferred_element_type=jnp.float32
    )
    return result.astype(jnp.bfloat16).reshape(layout)


def on_device(
    tokens,
    conv_gain,
    w_expand,
    dw_kernel,
    w_project,
    block_gain,
    block_qkv,
    block_out,
    grid_gain,
    grid_qkv,
    grid_out,
):
    tile_rows, tile_cols, channels = tokens.shape
    band_count = lax.axis_size("ns")
    strip_count = lax.axis_size("ew")
    bordered = with_halo(tokens, (("ns", 0), ("ew", 1)), 1)
    hidden = expand_rows(bordered, conv_gain, w_expand)
    row_place = lax.axis_index("ns") * tile_rows - 1 + jnp.arange(tile_rows + 2, dtype=jnp.int32)
    col_place = lax.axis_index("ew") * tile_cols - 1 + jnp.arange(tile_cols + 2, dtype=jnp.int32)
    row_inside = (row_place >= 0) & (row_place < tile_rows * band_count)
    col_inside = (col_place >= 0) & (col_place < tile_cols * strip_count)
    inside = row_inside[:, None] & col_inside[None, :]
    padded = jnp.where(inside[:, :, None], hidden, jnp.zeros_like(hidden))
    active = depthwise(padded, dw_kernel, tile_rows, tile_cols)
    update = jnp.dot(
        active.reshape(-1, active.shape[-1]), w_project, preferred_element_type=jnp.float32
    )
    after_conv = (
        tokens.astype(jnp.float32) + update.reshape(tile_rows, tile_cols, channels)
    ).astype(jnp.bfloat16)
    shaped = after_conv.reshape(tile_rows, tile_cols // WINDOW, WINDOW, 1, channels)
    after_block = attend(shaped, block_gain, block_qkv, block_out)
    stride_cols = tile_cols * strip_count // WINDOW
    per_strip = WINDOW // strip_count
    shared = stride_cols // band_count
    local_rows = tile_rows // strip_count
    sectioned = after_block.reshape(1, tile_rows, per_strip, stride_cols, channels)
    grouped = joined_exchange(sectioned, ("ns", "ew"), ("ns", "ew"), (3, 1), (0, 2))
    windows = grouped.reshape(WINDOW, band_count // WINDOW * local_rows, WINDOW, shared, channels)
    attended = attend(windows, grid_gain, grid_qkv, grid_out)
    attended = attended.reshape(band_count, local_rows, WINDOW, shared, channels)
    returned = joined_exchange(attended, ("ns", "ew"), ("ns", "ew"), (0, 2), (3, 1))
    return returned.reshape(tile_rows, tile_cols, channels)


def solution(mesh):
    in_specs = (P("ns", "ew", None), P(), P(), P(), P(), P(), P(), P(), P(), P(), P())
    out_specs = P("ns", "ew", None)
    return jax.shard_map(
        on_device, mesh=mesh, in_specs=in_specs, out_specs=out_specs, check_vma=False
    )
```

profile of v0, /device:TPU:1, one launch (start us, length us, event | category | flops | bytes accessed | tf_op | source)
XLA Modules:
  0.0 323.7 jit_solution(1281214865499387177)
XLA Ops:
  0.0 1.8 fusion.61
  1.8 1.3 collective-permute-start.1
  3.1 5.2 %collective-permute-start = (bf16[1,128,512]{2,1,0:T(8,128)(2,1)S(1)}, bf16[1,128,512]{2,1,0:T(8,128)(2,1)}, u32[]{:S(2)}, u32[]{:S(2)}) collective-permute-start(bf16[1,128,512]{2,1,0:T(8,128)(2,1)S(1)} %get-tuple-element.8), channel_id=1, source_target_pairs={{0,4},{4,8},{8,12},{12,16},{16,20},{20,24},{24,28},{28,32},{32,36}... | collective-permute-start | bytes 393224 | tf_op jit(solution)/shard_map/ppermute | solution.py:15
  8.3 1.6 fusion.62
  10.4 0.9 constant_dynamic-update-slice_fusion.2
  11.4 1.3 constant_dynamic-update-slice_fusion.1
  12.8 10.2 %collective-permute-start.2 = (bf16[10,1,512]{2,1,0:T(2,128)(2,1)S(1)}, bf16[10,1,512]{2,1,0:T(2,128)(2,1)S(1)}, u32[]{:S(2)}, u32[]{:S(2)}) collective-permute-start(bf16[10,1,512]{2,1,0:T(2,128)(2,1)S(1)} %get-tuple-element.5), channel_id=1, source_target_pairs={{0,1},{1,2},{2,3},{4,5},{5,6},{6,7},{8,9},{9,10},{10,11},{12,13},{... | collective-permute-start | bytes 30728 | tf_op jit(solution)/shard_map/ppermute | solution.py:15
  23.0 1.9 collective-permute-start.3
  25.6 6.4 %collective-permute-done.3 = bf16[10,1,512]{2,1,0:T(2,128)(2,1)S(1)} collective-permute-done((bf16[10,1,512]{2,1,0:T(2,128)(2,1)S(1)}, bf16[10,1,512]{2,1,0:T(2,128)(2,1)S(1)}, u32[]{:S(2)}, u32[]{:S(2)}) %collective-permute-start.3) | collective-permute-done | bytes 10272 | tf_op jit(solution)/shard_map/ppermute | solution.py:18
  32.6 1.3 multiply_reduce_fusion.2
  34.0 2.0 maximum_convert_fusion
  36.0 3.9 %reshape.259 = f32[1300,512]{1,0:T(8,128)} reshape(f32[10,130,512]{2,1,0:T(8,128)} %maximum_convert_fusion) | data formatting | bytes 5324800 | tf_op jit(solution)/shard_map/convert_element_type | solution.py:47
  39.9 8.4 %fusion.9 = bf16[1300,2048]{1,0:T(8,128)(2,1)} fusion(bf16[512,2048]{1,0:T(8,128)(2,1)S(1)} %copy-done, f32[1300,512]{1,0:T(8,128)} %reshape.259, f32[512]{0:T(512)S(1)} %copy-done.15, f32[1300]{0:T(1024)S(1)} %rsqrt.34, f32[1300]{0:T(1024)S(1)} %div.41), kind=kOutput, calls=%fused_computation.13 | convolution fusion | flops 2752921600 | bytes 10096800 | tf_op jit(solution)/shard_map/dot_general | solution.py:56
  48.3 5.4 %reshape.249 = bf16[10,130,2048]{2,1,0:T(8,128)(2,1)} reshape(bf16[1300,2048]{1,0:T(8,128)(2,1)} %fusion.9) | data formatting | bytes 10649600 | tf_op jit(solution)/shard_map/reshape | solution.py:57
  53.8 3.1 broadcast_select_fusion
  57.0 13.6 %convert_reduce_fusion = (f32[8,128]{1,0:T(8,128)S(1)}, bf16[8,128,512]{2,1,0:T(8,128)(2,1)S(1)}) fusion(bf16[2048,512]{1,0:T(8,128)(2,1)} %param.15, bf16[10,130,2048]{2,1,0:T(8,128)(2,1)S(1)} %broadcast_select_fusion, f32[2048]{0:T(1024)S(1)} %bitcast.130, f32[2048]{0:T(1024)S(1)} %bitcast.131, f32[2048]{0:T(1024)S(1)} %bitcast.124, ...), kind=kOutput, calls=%fused_computation.52 | convolution fusion | flops 2223504384 | bytes 42020864 | tf_op jit(solution)/shard_map/dot_general | solution.py:127
  71.6 4.9 %convolution_convert_fusion.1 = bf16[1024,1536]{1,0:T(8,128)(2,1)} fusion(bf16[1024,512]{1,0:T(8,128)(2,1)S(1)} %fusion.36, bf16[512,1536]{1,0:T(8,128)(2,1)} %param.17), kind=kOutput, calls=%fused_computation.45 | convolution fusion | flops 1612185600 | bytes 5767168 | tf_op jit(solution)/shard_map/dot_general | solution.py:79
  76.5 14.6 %reshape.250 = bf16[8,16,8,1,3,16,32]{6,5,4,2,1,0,3:T(8,128)(2,1)} reshape(bf16[1024,1536]{1,0:T(8,128)(2,1)} %convolution_convert_fusion.1) | data formatting | bytes 6291456 | tf_op jit(solution)/shard_map/reshape | solution.py:80
  91.0 8.8 %copy.115 = bf16[8,16,8,1,3,16,32]{6,2,0,5,1,3,4:T(8,128)(2,1)S(1)} copy(bf16[8,16,8,1,3,16,32]{6,5,4,2,1,0,3:T(8,128)(2,1)} %reshape.250) | data formatting | bytes 6291456 | tf_op jit(solution)/shard_map/reshape | solution.py:80
  99.8 6.3 %fusion.27 = f32[16,16,64,64]{2,3,1,0:T(8,128)} fusion(bf16[3,16,1,16,8,8,32]{6,5,4,3,1,2,0:T(8,128)(2,1)S(1)} %bitcast.110), kind=kOutput, calls=%fused_computation.39 | convolution fusion | flops 67108864 | bytes 12582912 | tf_op jit(solution)/shard_map/nhqd,nhkd->nhqk/dot_general | solution.py:87
  106.1 0.9 copy-done.2
  107.0 11.6 %fusion.63 = (f32[16,16,64]{2,1,0:T(8,128)S(1)}, f32[16,16,64,64]{2,3,1,0:T(8,128)}) fusion(f32[16,16,64,64]{2,3,1,0:T(8,128)} %fusion.27), kind=kOutput, calls=%fused_computation.97 | output fusion | flops 4194367 | bytes 8454144 | tf_op jit(solution)/shard_map/sub | solution.py:90
  118.6 7.2 %fusion.39 = bf16[16,16,64,32]{2,3,1,0:T(8,128)(2,1)} fusion(bf16[3,16,1,16,8,8,32]{6,5,4,3,1,2,0:T(8,128)(2,1)} %bitcast.111, f32[16,16,64,64]{2,3,1,0:T(8,128)} %get-tuple-element.23, f32[16,16,64]{2,1,0:T(8,128)S(1)} %get-tuple-element.22), kind=kOutput, calls=%fused_computation.64 | convolution fusion | flops 69730304 | bytes 13697024 | tf_op jit(solution)/shard_map/nhqk,nhkd->nhqd/dot_general | solution.py:91
  125.8 5.2 %copy.84 = bf16[16,16,64,32]{3,2,1,0:T(8,128)(2,1)} copy(bf16[16,16,64,32]{2,3,1,0:T(8,128)(2,1)} %fusion.39) | data formatting | bytes 2097152 | tf_op jit(solution)/shard_map/convert_element_type | solution.py:93
  131.0 9.0 %copy.85 = bf16[8,16,8,1,16,32]{5,4,2,1,0,3:T(8,128)(2,1)} copy(bf16[8,16,8,1,16,32]{5,2,0,4,1,3:T(8,128)(2,1)} %bitcast.117) | data formatting | bytes 2097152 | tf_op jit(solution)/shard_map/transpose | solution.py:95
  140.0 6.0 %reshape.252 = bf16[1024,512]{1,0:T(8,128)(2,1)S(1)} reshape(bf16[8,16,8,1,16,32]{5,4,2,1,0,3:T(8,128)(2,1)} %copy.85) | data formatting | bytes 2097152 | tf_op jit(solution)/shard_map/reshape | solution.py:95
  146.7 1.1 copy.86
  147.8 45.1 %all_to_all.10 = bf16[256,1,2,2,1,512]{5,3,2,4,1,0:T(2,128)(2,1)S(1)} all-to-all(bf16[256,1,2,2,1,512]{5,3,2,4,1,0:T(2,128)(2,1)S(1)} %bitcast.119), channel_id=1, replica_groups=mesh['ns'=64,'ew'=4] {'ns','ew'}, dimensions={0} | all-to-all | bytes 2097152 | tf_op jit(solution)/shard_map/all_to_all | solution.py:41
  192.9 1.2 fusion.48
  194.7 2.2 convert_bitcast_fusion
  196.9 2.3 multiply_reduce_fusion.3
  200.0 4.0 %copy.88 = f32[64,2,4,2,1,512]{5,3,2,1,0,4:T(2,128)} copy(f32[64,2,4,2,1,512]{5,3,1,2,0,4:T(2,128)} %convert_bitcast_fusion) | data formatting | bytes 4194304 | tf_op jit(solution)/shard_map/convert_element_type | solution.py:96
  204.1 2.7 reshape.261
  206.8 5.7 %convolution_convert_fusion = bf16[1024,1536]{1,0:T(8,128)(2,1)} fusion(bf16[512,1536]{1,0:T(8,128)(2,1)} %param.20, f32[1024,512]{1,0:T(8,128)S(1)} %reshape.261, f32[512]{0:T(512)S(1)} %copy-done.16, f32[1024]{0:T(1024)S(1)} %rsqrt.38, f32[1024]{0:T(1024)S(1)} %div.49), kind=kOutput, calls=%fused_computation.44 | convolution fusion | flops 1614282752 | bytes 6825984 | tf_op jit(solution)/shard_map/dot_general | solution.py:79
  212.5 14.6 %reshape.254 = bf16[8,16,8,1,3,16,32]{6,5,4,2,1,0,3:T(8,128)(2,1)} reshape(bf16[1024,1536]{1,0:T(8,128)(2,1)} %convolution_convert_fusion) | data formatting | bytes 6291456 | tf_op jit(solution)/shard_map/reshape | solution.py:80
  227.0 9.0 %copy.114 = bf16[8,16,8,1,3,16,32]{6,2,0,5,1,3,4:T(8,128)(2,1)S(1)} copy(bf16[8,16,8,1,3,16,32]{6,5,4,2,1,0,3:T(8,128)(2,1)} %reshape.254) | data formatting | bytes 6291456 | tf_op jit(solution)/shard_map/reshape | solution.py:80
  236.0 6.3 %fusion.25 = f32[16,16,64,64]{2,3,1,0:T(8,128)} fusion(bf16[3,16,1,16,8,8,32]{6,5,4,3,1,2,0:T(8,128)(2,1)S(1)} %bitcast.112), kind=kOutput, calls=%fused_computation.34 | convolution fusion | flops 67108864 | bytes 12582912 | tf_op jit(solution)/shard_map/nhqd,nhkd->nhqk/dot_general | solution.py:87
  242.3 0.9 copy-done.3
  243.2 11.6 %fusion.64 = (f32[16,16,64]{2,1,0:T(8,128)S(1)}, f32[16,16,64,64]{2,3,1,0:T(8,128)}) fusion(f32[16,16,64,64]{2,3,1,0:T(8,128)} %fusion.25), kind=kOutput, calls=%fused_computation.98 | output fusion | flops 4194367 | bytes 8454144 | tf_op jit(solution)/shard_map/sub | solution.py:90
  254.8 5.9 %fusion.40 = bf16[16,16,64,32]{2,3,1,0:T(8,128)(2,1)S(1)} fusion(bf16[3,16,1,16,8,8,32]{6,5,4,3,1,2,0:T(8,128)(2,1)} %bitcast.113, f32[16,16,64,64]{2,3,1,0:T(8,128)} %get-tuple-element.25, f32[16,16,64]{2,1,0:T(8,128)S(1)} %get-tuple-element.24), kind=kOutput, calls=%fused_computation.65 | convolution fusion | flops 69730304 | bytes 13697024 | tf_op jit(solution)/shard_map/nhqk,nhkd->nhqd/dot_general | solution.py:91
  260.7 3.2 copy.99
  264.0 9.0 %copy.100 = bf16[8,16,8,1,16,32]{5,4,2,1,0,3:T(8,128)(2,1)} copy(bf16[8,16,8,1,16,32]{5,2,0,4,1,3:T(8,128)(2,1)} %bitcast.118) | data formatting | bytes 2097152 | tf_op jit(solution)/shard_map/transpose | solution.py:95
  273.0 6.2 %reshape.256 = bf16[1024,512]{1,0:T(8,128)(2,1)S(1)} reshape(bf16[8,16,8,1,16,32]{5,4,2,1,0,3:T(8,128)(2,1)} %copy.100) | data formatting | bytes 2097152 | tf_op jit(solution)/shard_map/reshape | solution.py:95
  279.2 3.6 %add_convert_fusion = bf16[1024,512]{1,0:T(8,128)(2,1)} fusion(f32[1024,512]{1,0:T(8,128)} %copy-done.4, bf16[1024,512]{1,0:T(8,128)(2,1)S(1)} %reshape.256, bf16[512,512]{1,0:T(8,128)(2,1)} %param.21), kind=kOutput, calls=%fused_computation.60 | convolution fusion | flops 537919488 | bytes 4718592 | tf_op jit(solution)/shard_map/dot_general | solution.py:96
  282.7 1.5 reshape_reshape_reshape_reshape.3
  284.2 0.9 copy.101
  285.1 36.8 %all_to_all.11 = bf16[256,1,2,2,1,512]{5,3,2,4,1,0:T(2,128)(2,1)S(1)} all-to-all(bf16[256,1,2,2,1,512]{5,3,2,4,1,0:T(2,128)(2,1)S(1)} %bitcast.120), channel_id=1, replica_groups=mesh['ns'=64,'ew'=4] {'ns','ew'}, dimensions={0} | all-to-all | bytes 2097152 | tf_op jit(solution)/shard_map/all_to_all | solution.py:41
  321.9 1.5 copy.103
  (59 shorter events, 5.1 us)
Async XLA Ops:
  0.0 39.9 %copy-start = (bf16[512,2048]{1,0:T(8,128)(2,1)S(1)}, bf16[512,2048]{1,0:T(8,128)(2,1)}, u32[]{:S(2)}) copy-start(bf16[512,2048]{1,0:T(8,128)(2,1)} %param.13) | copy-start | bytes 6291460
  1.8 10.9 %collective-permute-start.1 = (bf16[1,128,512]{2,1,0:T(8,128)(2,1)}, bf16[1,128,512]{2,1,0:T(8,128)(2,1)S(1)}, u32[]{:S(2)}, u32[]{:S(2)}) collective-permute-start(bf16[1,128,512]{2,1,0:T(8,128)(2,1)} %get-tuple-element.7), channel_id=1, source_target_pairs={{4,0},{8,4},{12,8},{16,12},{20,16},{24,20},{28,24},{32,28},{36,32}... | collective-permute-start | bytes 393224 | tf_op jit(solution)/shard_map/ppermute | solution.py:18
  3.1 7.4 %collective-permute-start = (bf16[1,128,512]{2,1,0:T(8,128)(2,1)S(1)}, bf16[1,128,512]{2,1,0:T(8,128)(2,1)}, u32[]{:S(2)}, u32[]{:S(2)}) collective-permute-start(bf16[1,128,512]{2,1,0:T(8,128)(2,1)S(1)} %get-tuple-element.8), channel_id=1, source_target_pairs={{0,4},{4,8},{8,12},{12,16},{16,20},{20,24},{24,28},{28,32},{32,36}... | collective-permute-start | bytes 393224 | tf_op jit(solution)/shard_map/ppermute | solution.py:15
  12.8 12.8 %collective-permute-start.2 = (bf16[10,1,512]{2,1,0:T(2,128)(2,1)S(1)}, bf16[10,1,512]{2,1,0:T(2,128)(2,1)S(1)}, u32[]{:S(2)}, u32[]{:S(2)}) collective-permute-start(bf16[10,1,512]{2,1,0:T(2,128)(2,1)S(1)} %get-tuple-element.5), channel_id=1, source_target_pairs={{0,1},{1,2},{2,3},{4,5},{5,6},{6,7},{8,9},{9,10},{10,11},{12,13},{... | collective-permute-start | bytes 30728 | tf_op jit(solution)/shard_map/ppermute | solution.py:15
  23.0 9.0 %collective-permute-start.3 = (bf16[10,1,512]{2,1,0:T(2,128)(2,1)S(1)}, bf16[10,1,512]{2,1,0:T(2,128)(2,1)S(1)}, u32[]{:S(2)}, u32[]{:S(2)}) collective-permute-start(bf16[10,1,512]{2,1,0:T(2,128)(2,1)S(1)} %get-tuple-element.6), channel_id=1, source_target_pairs={{1,0},{2,1},{3,2},{5,4},{6,5},{7,6},{9,8},{10,9},{11,10},{13,12},{... | collective-permute-start | bytes 30728 | tf_op jit(solution)/shard_map/ppermute | solution.py:18
  33.9 5.9 %copy-start.15 = (f32[512]{0:T(512)S(1)}, f32[512]{0:T(512)}, u32[]{:S(2)}) copy-start(f32[512]{0:T(512)} %param.12) | copy-start | bytes 6148
  53.7 3.2 copy-start.5
  53.7 3.2 copy-start.6
  53.7 3.2 copy-start.7
  53.7 3.2 copy-start.8
  53.7 3.2 copy-start.9
  53.7 3.2 copy-start.10
  53.7 3.2 copy-start.11
  53.8 3.2 copy-start.12
  57.0 14.2 %copy-start.13 = (f32[512]{0:T(512)S(1)}, f32[512]{0:T(512)}, u32[]{:S(2)}) copy-start(f32[512]{0:T(512)} %param.16) | copy-start | bytes 6148
  99.8 7.2 %copy-start.2 = (bf16[8,16,8,1,3,16,32]{6,2,0,5,1,3,4:T(8,128)(2,1)}, bf16[8,16,8,1,3,16,32]{6,2,0,5,1,3,4:T(8,128)(2,1)S(1)}, u32[]{:S(2)}) copy-start(bf16[8,16,8,1,3,16,32]{6,2,0,5,1,3,4:T(8,128)(2,1)S(1)} %copy.115) | copy-start | bytes 9437188
  140.0 6.0 %copy-start.14 = (bf16[512,512]{1,0:T(8,128)(2,1)S(1)}, bf16[512,512]{1,0:T(8,128)(2,1)}, u32[]{:S(2)}) copy-start(bf16[512,512]{1,0:T(8,128)(2,1)} %param.18) | copy-start | bytes 1572868
  200.0 6.7 %copy-start.16 = (f32[512]{0:T(512)S(1)}, f32[512]{0:T(512)}, u32[]{:S(2)}) copy-start(f32[512]{0:T(512)} %param.19) | copy-start | bytes 6148
  206.8 5.7 %copy-start.4 = (f32[1024,512]{1,0:T(8,128)}, f32[1024,512]{1,0:T(8,128)S(1)}, u32[]{:S(2)}) copy-start(f32[1024,512]{1,0:T(8,128)S(1)} %reshape.261) | copy-start | bytes 6291460
  236.0 7.2 %copy-start.3 = (bf16[8,16,8,1,3,16,32]{6,2,0,5,1,3,4:T(8,128)(2,1)}, bf16[8,16,8,1,3,16,32]{6,2,0,5,1,3,4:T(8,128)(2,1)S(1)}, u32[]{:S(2)}) copy-start(bf16[8,16,8,1,3,16,32]{6,2,0,5,1,3,4:T(8,128)(2,1)S(1)} %copy.114) | copy-start | bytes 9437188
  279.2 44.3 %copy-start.1 = (bf16[512,2048]{1,0:T(8,128)(2,1)S(1)}, bf16[512,2048]{1,0:T(8,128)(2,1)}, u32[]{:S(2)}) copy-start(bf16[512,2048]{1,0:T(8,128)(2,1)} %param.13) | copy-start | bytes 6291460
where the time goes:
time: 328 us; the launch traced here: 324 us
  local copies, waits for them, and re-layouts  116 us (35%)
  blocking collectives  81.8 us (25%)
  matrix products  62.6 us (19%)
  other arithmetic  37.8 us (12%)
  starting transfers between devices  18.6 us (6%)
  waiting for transfers between devices  6.41 us (2%)
    all_to_all x2, blocking collectives, joined_exchange(): tiles = lax.all_to_all(tiles, axis, split_axis=0, concat_axis=0, tiled=True)  81.8 us
    reshape x4, local copies, waits for them, and re-layouts, attend(): packed = packed.reshape(dim_p, dim_w, dim_q, dim_s, 3, HEADS, head_dim)  46.8 us
    sub x2, other arithmetic, attend(): weights = jax.nn.softmax(scores, axis=-1).astype(jnp.bfloat16)  23.2 us
    transpose x2, local copies, waits for them, and re-layouts, attend(): blended = jnp.transpose(blended, (3, 0, 4, 1, 2, 5)).reshape(-1, channels)  18 us
    ppermute x2, starting transfers between devices, with_halo(): lax.ppermute(lax.slice_in_dim(block, block.shape[dim] - width, None, axis...  15.4 us
    dot_general x1, matrix products, on_device(): jnp.dot(active.reshape(-1, active.shape[-1]), w_project, preferred_elemen...  13.6 us
    dot_general x2, matrix products, attend(): jnp.einsum('nhqk,nhkd->nhqd', weights, value_rows, preferred_element_type...  13.1 us
    dot_general x2, matrix products, attend(): jnp.einsum('nhqd,nhkd->nhqk', queries, key_rows, preferred_element_type=j...  12.5 us
  transfers between devices with their start and end apart: 4, of which 1 were waited for; matrix products, arithmetic and copies ran while one was open for 2% of the time, Pallas kernels for 0%

commit v1 on v0

v1 whole, which is shorter than its diff:
```python
import functools
import math

import jax
import jax.numpy as jnp
from jax import lax
from jax.experimental import pallas as pl
from jax.experimental.pallas import tpu as pltpu
from jax.sharding import PartitionSpec as P

MESH = pl.DeviceIdType.MESH
BF = jnp.bfloat16
F32 = jnp.float32
HEADS = 16
EXP_SCALE = math.log2(math.e) / math.sqrt(32.0)
GELU_A = math.sqrt(2.0 / math.pi)
GELU_B = GELU_A * 0.044715


def gelu(x):
    half = 0.5 * x
    t = jnp.tanh(x * (GELU_A + GELU_B * (x * x)))
    return half + half * t


def layer_norm(x, gain):
    center = x - jnp.mean(x, axis=-1, keepdims=True)
    spread = jnp.mean(center * center, axis=-1, keepdims=True)
    return (center * lax.rsqrt(spread + 1e-05) * gain).astype(BF)


def dot(a, b):
    return jnp.dot(a, b, preferred_element_type=F32)


def head_mask(head):
    lane = lax.broadcasted_iota(jnp.int32, (1, 128), 1)
    return (lane >= head * 32) & (lane < head * 32 + 32)


def attend_window(qkv, row, heads_out, out_row):
    zero = jnp.zeros((64, 128), BF)
    one = jnp.ones((64, 128), BF)
    low = lax.broadcasted_iota(jnp.int32, (1, 128), 1) < 64
    for group in range(4):
        lanes = 128 * group
        q = qkv[pl.ds(row, 64), lanes : lanes + 128]
        k = qkv[pl.ds(row, 64), 512 + lanes : 512 + lanes + 128]
        v = qkv[pl.ds(row, 64), 1024 + lanes : 1024 + lanes + 128]
        masks = [jnp.broadcast_to(head_mask(h), (64, 128)) for h in range(4)]
        keys = jnp.concatenate([jnp.where(m, k, zero) for m in masks], axis=0)
        values = jnp.concatenate([jnp.where(m, v, zero) for m in masks], axis=0)
        ones = jnp.concatenate([jnp.where(m, one, zero) for m in masks], axis=0)
        scores = lax.dot_general(q, keys, (((1,), (1,)), ((), ())), preferred_element_type=F32)
        parts = []
        for t in range(2):
            s = scores[:, 128 * t : 128 * t + 128]
            top_low = jnp.max(jnp.where(low, s, -jnp.inf), axis=1, keepdims=True)
            top_high = jnp.max(jnp.where(low, -jnp.inf, s), axis=1, keepdims=True)
            top = jnp.where(low, top_low, top_high)
            parts.append(jnp.exp2((s - top) * EXP_SCALE).astype(BF))
        weights = jnp.concatenate(parts, axis=1)
        both = dot(weights, jnp.concatenate([values, ones], axis=1))
        heads_out[pl.ds(out_row, 64), lanes : lanes + 128] = (both[:, :128] / both[:, 128:]).astype(BF)


def kernel(
    tok_hbm, conv_gain, we_hbm, dw, wp_hbm, block_gain, bqkv_hbm, bo_hbm, grid_gain, gqkv_hbm, go_hbm,
    out,
    tok, we, wp, bqkv, bo, gqkv, go,
    halo_n, halo_s, halo_w, halo_e,
    normed, normed_halo, normed_edge, expanded, acc, packed, heads_out, send1, recv1, send2, perm, unperm,
    weight_sem, halo_send, halo_recv, send1_sem, recv1_sem, send2_sem, recv2_sem, local_sem,
):
    n = lax.axis_index("ns")
    e = lax.axis_index("ew")
    a_me = n // 8
    rho = n % 8
    me = a_me * 4 + e
    north, south = (n + 63) % 64, (n + 1) % 64
    west, east = (e + 3) % 4, (e + 1) % 4

    def device(p):
        return (p // 4 * 8 + rho, p % 4)

    barrier = pltpu.get_barrier_semaphore()

    def greet(k, c):
        pl.semaphore_signal(barrier, inc=1, device_id=device((me + k) % 32), device_id_type=MESH)
        return c

    lax.fori_loop(1, 32, greet, 0)
    for row_band in (north, south):
        for strip in (west, e, east):
            pl.semaphore_signal(barrier, inc=1, device_id=(row_band, strip), device_id_type=MESH)

    loads = [
        pltpu.make_async_copy(src, dst, weight_sem.at[i])
        for i, (src, dst) in enumerate(
            [(tok_hbm, tok), (we_hbm, we), (wp_hbm, wp), (bqkv_hbm, bqkv), (bo_hbm, bo), (gqkv_hbm, gqkv), (go_hbm, go)]
        )
    ]
    for load in loads:
        load.start()
    pl.semaphore_wait(barrier, 37)

    moves = [
        (tok_hbm.at[0], halo_s, (north, e)),
        (tok_hbm.at[7], halo_n, (south, e)),
        (tok_hbm.at[:, 0:8], halo_e.at[1:9], (n, west)),
        (tok_hbm.at[:, 120:128], halo_w.at[1:9], (n, east)),
        (tok_hbm.at[0, 0:8], halo_e.at[9], (north, west)),
        (tok_hbm.at[0, 120:128], halo_w.at[9], (north, east)),
        (tok_hbm.at[7, 0:8], halo_e.at[0], (south, west)),
        (tok_hbm.at[7, 120:128], halo_w.at[0], (south, east)),
    ]
    halos = [
        pltpu.make_async_remote_copy(
            src_ref=src, dst_ref=dst, send_sem=halo_send.at[i], recv_sem=halo_recv.at[i], device_id=to, device_id_type=MESH
        )
        for i, (src, dst, to) in enumerate(moves)
    ]
    for halo in halos:
        halo.start()

    loads[0].wait()
    gain = conv_gain[...]
    for i in range(8):
        normed[i * 128 : i * 128 + 128, :] = layer_norm(tok[i].astype(F32), gain)
    loads[1].wait()

    def expand_own(f, c):
        cols = pl.ds(pl.multiple_of(f * 256, 256), 256)
        for pair in range(4):
            hidden = gelu(dot(normed[pair * 256 : pair * 256 + 256, :], we[:, cols]))
            for r in range(2):
                for t in range(2):
                    expanded[2 * f + t, 1 + pair * 2 + r, 8:136, :] = hidden[r * 128 : r * 128 + 128, 128 * t : 128 * t + 128]
        return c

    lax.fori_loop(0, 8, expand_own, 0)

    row = lax.broadcasted_iota(jnp.int32, (256, 256), 0)
    col = lax.broadcasted_iota(jnp.int32, (256, 256), 1)
    perm[...] = jnp.where(col == (row & 31) * 8 + (row >> 5), 1.0, 0.0).astype(BF)
    unperm[...] = jnp.where(col == (row & 7) * 32 + (row >> 3), 1.0, 0.0).astype(BF)

    for halo in halos:
        halo.wait()
    zero_row = jnp.zeros((128, 512), BF)
    normed_halo[0:128, :] = jnp.where(n > 0, layer_norm(halo_n[...].astype(F32), gain), zero_row)
    normed_halo[128:256, :] = jnp.where(n < 63, layer_norm(halo_s[...].astype(F32), gain), zero_row)
    pick = lax.broadcasted_iota(jnp.int32, (16, 80), 1) - 8 * lax.broadcasted_iota(jnp.int32, (16, 80), 0)
    edge_row = lax.broadcasted_iota(jnp.int32, (16, 512), 0)
    rows_in = ((edge_row > 0) | (n > 0)) & ((edge_row < 9) | (n < 63))
    for side, (block, at, there) in enumerate([(halo_w, 7, e > 0), (halo_e, 0, e < 3)]):
        chosen = jnp.where(pick == at, 1.0, 0.0).astype(BF)
        tokens_edge = dot(chosen, block[...].reshape(80, 512))
        ned = layer_norm(tokens_edge, gain).astype(F32)
        normed_edge[side * 16 : side * 16 + 16, :] = jnp.where(rows_in & there, ned, 0.0).astype(BF)

    def expand_halo(f, c):
        cols = pl.ds(pl.multiple_of(f * 256, 256), 256)
        hidden = gelu(dot(normed_halo[...], we[:, cols]))
        edge = gelu(dot(normed_edge[...], we[:, cols]))
        for t in range(2):
            lanes = slice(128 * t, 128 * t + 128)
            expanded[2 * f + t, 0, 8:136, :] = hidden[0:128, lanes]
            expanded[2 * f + t, 9, 8:136, :] = hidden[128:256, lanes]
            for r in range(10):
                expanded[2 * f + t, r, 7:8, :] = edge[r : r + 1, lanes]
                expanded[2 * f + t, r, 136:137, :] = edge[16 + r : 17 + r, lanes]
        return c

    lax.fori_loop(0, 8, expand_halo, 0)
    for load in loads[2:]:
        load.wait()

    for quarter in range(4):

        def conv(f, c, quarter=quarter):
            pieces = []
            for t in range(4):
                lane_tile = 4 * f + t
                lanes = pl.ds(pl.multiple_of(f * 512 + t * 128, 128), 128)
                taps = [[dw[a, b : b + 1, lanes] for b in range(3)] for a in range(3)]
                rows = [[None, None] for _ in range(8)]
                for seg in range(2):
                    start = 64 * seg + 16 * quarter + 7
                    loaded = [
                        [expanded[lane_tile, r, start + b : start + b + 16, :] for b in range(3)] for r in range(10)
                    ]
                    for i in range(8):
                        total = None
                        for a in range(3):
                            for b in range(3):
                                term = loaded[i + a][b] * taps[a][b]
                                total = term if total is None else total + term
                        rows[i][seg] = gelu(total).astype(BF)
                pieces.append(jnp.concatenate([rows[i][s] for i in range(8) for s in range(2)], axis=0))
            active = jnp.concatenate(pieces, axis=1)
            update = dot(active, wp[pl.ds(pl.multiple_of(f * 512, 512), 512), :])

            @pl.when(f == 0)
            def _():
                acc[...] = update

            @pl.when(f > 0)
            def _():
                acc[...] += update

            return c

        lax.fori_loop(0, 4, conv, 0)
        windows = []
        for seg in range(2):
            for j2 in range(2):
                for i in range(8):
                    c0 = 16 * quarter + 8 * j2
                    windows.append(
                        acc[i * 32 + seg * 16 + 8 * j2 : i * 32 + seg * 16 + 8 * j2 + 8, :]
                        + tok[i, 64 * seg + c0 : 64 * seg + c0 + 8, :].astype(F32)
                    )
        x = jnp.concatenate(windows, axis=0).astype(BF).astype(F32)
        acc[...] = x
        packed[0:256, :] = dot(layer_norm(x, block_gain[...]), bqkv[...]).astype(BF)

        def window(w, c):
            at = pl.multiple_of(w * 64, 64)
            attend_window(packed, at, heads_out, at)
            return c

        lax.fori_loop(0, 4, window, 0)
        acc[...] += dot(heads_out[0:256, :], bo[...])
        for j2 in range(2):
            j = 2 * quarter + j2
            ordered = []
            for i in range(8):
                for seg in range(2):
                    r0 = ((seg * 2 + j2) * 8 + i) * 8
                    ordered.append(acc[r0 : r0 + 8, :])
            send1[j] = jnp.concatenate(ordered, axis=0).astype(BF).reshape(8, 2, 8, 512)
            strip = (j % 2) * 2 + (j // 2) % 2
            half = j // 4

            def send(k, c, j=j, strip=strip, half=half):
                i = jnp.bitwise_xor(a_me, k)
                p = i * 4 + strip

                @pl.when(p != me)
                def _():
                    pltpu.make_async_remote_copy(
                        src_ref=send1.at[j, i],
                        dst_ref=recv1.at[half, me],
                        send_sem=send1_sem.at[j, i],
                        recv_sem=recv1_sem.at[half, me],
                        device_id=device(p),
                        device_id_type=MESH,
                    ).start()

                @pl.when(p == me)
                def _():
                    pltpu.make_async_copy(send1.at[j, i], recv1.at[half, me], local_sem.at[half]).start()

                return c

            lax.fori_loop(0, 8, send, 0)

    for half in range(2):

        def arrive(k, c, half=half):
            p = jnp.bitwise_xor(me, k)
            pltpu.make_async_remote_copy(
                src_ref=send1.at[0, 0],
                dst_ref=recv1.at[half, p],
                send_sem=send1_sem.at[0, 0],
                recv_sem=recv1_sem.at[half, p],
                device_id=device(p),
                device_id_type=MESH,
            ).wait_recv()
            return c

        lax.fori_loop(1, 32, arrive, 0)
        pltpu.make_async_copy(send1.at[0, 0], recv1.at[half, me], local_sem.at[half]).wait()
        for u in range(2):
            x = recv1[half, 16 * u : 16 * u + 16].reshape(256, 512)
            ordered = dot(perm[...], layer_norm(x.astype(F32), grid_gain[...])).astype(BF)
            packed_u = dot(ordered, gqkv[...]).astype(BF)
            for s in range(8):
                packed[s * 64 + 32 * u : s * 64 + 32 * u + 32, :] = packed_u[s * 32 : s * 32 + 32, :]

        def grid_window(w, c):
            at = pl.multiple_of(w * 64, 64)
            attend_window(packed, at, heads_out, at)
            return c

        lax.fori_loop(0, 8, grid_window, 0)
        place = 32 * half + 8 * ((e % 2) * 2 + e // 2)
        for u in range(2):
            mixed = jnp.concatenate([heads_out[s * 64 + 32 * u : s * 64 + 32 * u + 32, :] for s in range(8)], axis=0)
            natural = dot(unperm[...], mixed).astype(BF)
            x = recv1[half, 16 * u : 16 * u + 16].reshape(256, 512).astype(F32)
            result = x + dot(natural, go[...])
            send2[half, 16 * u : 16 * u + 16] = result.astype(BF).reshape(16, 2, 8, 512)

            def give_back(k, c, half=half, u=u):
                p = 16 * u + jnp.bitwise_xor(me % 16, k)
                target = out.at[a_me, :, pl.ds(pl.multiple_of(place, 8), 8), :]

                @pl.when(p != me)
                def _():
                    pltpu.make_async_remote_copy(
                        src_ref=send2.at[half, p],
                        dst_ref=target,
                        send_sem=send2_sem.at[half, p],
                        recv_sem=recv2_sem.at[half, me],
                        device_id=device(p),
                        device_id_type=MESH,
                    ).start()

                @pl.when(p == me)
                def _():
                    pltpu.make_async_copy(send2.at[half, p], target, local_sem.at[2 + half]).start()

                return c

            lax.fori_loop(0, 16, give_back, 0)

    def finish(q, c):
        half = q // 32
        p = q % 32
        i = p // 4
        strip = p % 4
        j = 4 * half + (strip % 2) * 2 + strip // 2
        place = 32 * half + 8 * ((strip % 2) * 2 + strip // 2)
        target = out.at[i, :, pl.ds(pl.multiple_of(place, 8), 8), :]

        @pl.when(p != me)
        def _():
            pltpu.make_async_remote_copy(
                src_ref=send1.at[j, i], dst_ref=recv1.at[half, p], send_sem=send1_sem.at[j, i],
                recv_sem=recv1_sem.at[half, p], device_id=device(p), device_id_type=MESH,
            ).wait_send()
            pltpu.make_async_remote_copy(
                src_ref=send2.at[half, p], dst_ref=target, send_sem=send2_sem.at[half, p],
                recv_sem=recv2_sem.at[half, p], device_id=device(p), device_id_type=MESH,
            ).wait()

        @pl.when(p == me)
        def _():
            pltpu.make_async_copy(send2.at[half, p], target, local_sem.at[2 + half]).wait()

        return c

    lax.fori_loop(0, 64, finish, 0)


def on_device(
    tokens, conv_gain, w_expand, dw_kernel, w_project, block_gain, block_qkv, block_out, grid_gain, grid_qkv, grid_out
):
    whole = pl.BlockSpec(memory_space=pltpu.VMEM)
    anywhere = pl.BlockSpec(memory_space=pl.ANY)
    result = pl.pallas_call(
        kernel,
        out_shape=jax.ShapeDtypeStruct((8, 2, 64, 512), BF),
        in_specs=[anywhere, whole, anywhere, whole, anywhere, whole, anywhere, anywhere, whole, anywhere, anywhere],
        out_specs=anywhere,
        scratch_shapes=[
            pltpu.VMEM((8, 128, 512), BF),
            pltpu.VMEM((512, 2048), BF),
            pltpu.VMEM((2048, 512), BF),
            pltpu.VMEM((512, 1536), BF),
            pltpu.VMEM((512, 512), BF),
            pltpu.VMEM((512, 1536), BF),
            pltpu.VMEM((512, 512), BF),
            pltpu.VMEM((128, 512), BF),
            pltpu.VMEM((128, 512), BF),
            pltpu.VMEM((10, 8, 512), BF),
            pltpu.VMEM((10, 8, 512), BF),
            pltpu.VMEM((1024, 512), BF),
            pltpu.VMEM((256, 512), BF),
            pltpu.VMEM((32, 512), BF),
            pltpu.VMEM((16, 10, 144, 128), F32),
            pltpu.VMEM((256, 512), F32),
            pltpu.VMEM((512, 1536), BF),
            pltpu.VMEM((512, 512), BF),
            pltpu.VMEM((8, 8, 2, 8, 512), BF),
            pltpu.VMEM((2, 32, 2, 8, 512), BF),
            pltpu.VMEM((2, 32, 2, 8, 512), BF),
            pltpu.VMEM((256, 256), BF),
            pltpu.VMEM((256, 256), BF),
            pltpu.SemaphoreType.DMA((7,)),
            pltpu.SemaphoreType.DMA((8,)),
            pltpu.SemaphoreType.DMA((8,)),
            pltpu.SemaphoreType.DMA((8, 8)),
            pltpu.SemaphoreType.DMA((2, 32)),
            pltpu.SemaphoreType.DMA((2, 32)),
            pltpu.SemaphoreType.DMA((2, 32)),
            pltpu.SemaphoreType.DMA((4,)),
        ],
        compiler_params=pltpu.CompilerParams(
            collective_id=0, has_side_effects=True, vmem_limit_bytes=60 * 1024 * 1024
        ),
        name="maxvit",
    )(
        tokens, conv_gain.reshape(1, 512), w_expand, dw_kernel, w_project, block_gain.reshape(1, 512), block_qkv, block_out,
        grid_gain.reshape(1, 512), grid_qkv, grid_out,
    )
    return result.reshape(tokens.shape)


def solution(mesh):
    in_specs = (P("ns", "ew", None), P(), P(), P(), P(), P(), P(), P(), P(), P(), P())
    out_specs = P("ns", "ew", None)
    return jax.shard_map(
        on_device, mesh=mesh, in_specs=in_specs, out_specs=out_specs, check_vma=False
    )
```

time: 328 us -> 84.7 us (0.26); the launches traced: 324 us -> 84.6 us
  local copies, waits for them, and re-layouts: 116 us -> 2.26 us
  Pallas kernels: 0 us -> 82.3 us
  blocking collectives: 81.8 us -> 0 us
  matrix products: 62.6 us -> 0 us
  other arithmetic: 37.8 us -> 0 us
  starting transfers between devices: 18.6 us -> 0 us
  waiting for transfers between devices: 6.41 us -> 0 us
    pallas_call x0 -> x1, Pallas kernels: none -> 82.3 us  [on_device(): pl.pallas_call(kernel, out_shape=jax.ShapeDtypeStruct((8, 2, 64, 512), BF...]
    all_to_all x2 -> x0, blocking collectives: 81.8 us -> none  [joined_exchange(): tiles = lax.all_to_all(tiles, axis, split_axis=0, concat_axis=0, tiled=True)]
    reshape x7 -> x0, local copies, waits for them, and re-layouts: 64.4 us -> none  [the longest x4 46.8 us: attend(): packed = packed.reshape(dim_p, dim_w, dim_q, dim_s, 3, HEADS, head_dim)]
    dot_general x10 -> x0, matrix products: 62.6 us -> none  [the longest x1 13.6 us: on_device(): jnp.dot(active.reshape(-1, active.shape[-1]), w_project, preferred_elemen...]
    sub x2 -> x0, other arithmetic: 23.2 us -> none  [attend(): weights = jax.nn.softmax(scores, axis=-1).astype(jnp.bfloat16)]
    transpose x3 -> x0, local copies, waits for them, and re-layouts: 19.6 us -> none  [the longest x2 18 us: attend(): blended = jnp.transpose(blended, (3, 0, 4, 1, 2, 5)).reshape(-1, channels)]
    convert_element_type x5 -> x0, local copies, waits for them, and re-layouts: 19.1 us -> none  [the longest x2 8.43 us: attend(): blended = jnp.einsum('nhqk,nhkd->nhqd', weights, value_rows, preferred_el...]
    ppermute x4 -> x0, starting transfers between devices: 18.6 us -> none  [the longest x2 15.4 us: with_halo(): lax.ppermute(lax.slice_in_dim(block, block.shape[dim] - width, None, axis...]
  transfers between devices with their start and end apart: 4 -> 0, of which waited for: 1 -> 0; matrix products, arithmetic and copies ran while one was open for 2% -> 0% of each run, Pallas kernels for 0% -> 0%
where the time goes in v1:
time: 84.7 us; the launch traced here: 84.6 us
  Pallas kernels  82.3 us (97%)
  local copies, waits for them, and re-layouts  2.26 us (3%)
    pallas_call x1, Pallas kernels, on_device(): pl.pallas_call(kernel, out_shape=jax.ShapeDtypeStruct((8, 2, 64, 512), BF...  82.3 us
    unnamed x1, local copies, waits for them, and re-layouts  2.26 us

profile of v1, /device:TPU:1, one launch (start us, length us, event | category | flops | bytes accessed | tf_op | source)
XLA Modules:
  0.0 84.6 jit_solution(5293294047460816971)
XLA Ops:
  0.0 82.3 %maxvit.1 = bf16[8,2,64,512]{3,2,1,0:T(8,128)(2,1)} custom-call(bf16[8,128,512]{2,1,0:T(8,128)(2,1)} %tok_hbm.1, f32[1,512]{1,0:T(1,128)} %bitcast.5, bf16[512,2048]{1,0:T(8,128)(2,1)} %we_hbm.1, f32[3,3,2048]{2,1,0:T(4,128)} %dw.1, bf16[2048,512]{1,0:T(8,128)(2,1)} %wp_hbm.1, f32[1,512]{1,0:T(1,128)} %bitcast.6, bf16[512,1536]{1,0:T(8,128)(2,1)} %bqkv_hbm.1, ...), custom_call_target="tpu_custom_call" | custom-call | tf_op jit(solution)/shard_map/maxvit/pallas_call | solution.py:363
  82.3 2.3 %copy.13 = bf16[8,128,512]{2,1,0:T(8,128)(2,1)} copy(bf16[8,128,512]{2,1,0:T(8,128)(2,1)} %bitcast.4) | data formatting | bytes 2097152

commit v2 on v1

--- a/solution.py
+++ b/solution.py
@@ -38,30 +38,34 @@
     return (lane >= head * 32) & (lane < head * 32 + 32)
 
 
-def attend_window(qkv, row, heads_out, out_row):
+def attend_windows(qkv, rows, heads_out):
     zero = jnp.zeros((64, 128), BF)
     one = jnp.ones((64, 128), BF)
     low = lax.broadcasted_iota(jnp.int32, (1, 128), 1) < 64
-    for group in range(4):
-        lanes = 128 * group
+    masks = [jnp.broadcast_to(head_mask(h), (64, 128)) for h in range(4)]
+    ones = jnp.concatenate([jnp.where(m, one, zero) for m in masks], axis=0)
+    jobs = [(row, 128 * group) for row in rows for group in range(4)]
+    scores = []
+    for row, lanes in jobs:
         q = qkv[pl.ds(row, 64), lanes : lanes + 128]
         k = qkv[pl.ds(row, 64), 512 + lanes : 512 + lanes + 128]
-        v = qkv[pl.ds(row, 64), 1024 + lanes : 1024 + lanes + 128]
-        masks = [jnp.broadcast_to(head_mask(h), (64, 128)) for h in range(4)]
         keys = jnp.concatenate([jnp.where(m, k, zero) for m in masks], axis=0)
-        values = jnp.concatenate([jnp.where(m, v, zero) for m in masks], axis=0)
-        ones = jnp.concatenate([jnp.where(m, one, zero) for m in masks], axis=0)
-        scores = lax.dot_general(q, keys, (((1,), (1,)), ((), ())), preferred_element_type=F32)
+        scores.append(lax.dot_general(q, keys, (((1,), (1,)), ((), ())), preferred_element_type=F32))
+    weights = []
+    for score in scores:
         parts = []
         for t in range(2):
-            s = scores[:, 128 * t : 128 * t + 128]
+            s = score[:, 128 * t : 128 * t + 128]
             top_low = jnp.max(jnp.where(low, s, -jnp.inf), axis=1, keepdims=True)
             top_high = jnp.max(jnp.where(low, -jnp.inf, s), axis=1, keepdims=True)
             top = jnp.where(low, top_low, top_high)
             parts.append(jnp.exp2((s - top) * EXP_SCALE).astype(BF))
-        weights = jnp.concatenate(parts, axis=1)
-        both = dot(weights, jnp.concatenate([values, ones], axis=1))
-        heads_out[pl.ds(out_row, 64), lanes : lanes + 128] = (both[:, :128] / both[:, 128:]).astype(BF)
+        weights.append(jnp.concatenate(parts, axis=1))
+    for (row, lanes), weight in zip(jobs, weights):
+        v = qkv[pl.ds(row, 64), 1024 + lanes : 1024 + lanes + 128]
+        values = jnp.concatenate([jnp.where(m, v, zero) for m in masks], axis=0)
+        both = dot(weight, jnp.concatenate([values, ones], axis=1))
+        heads_out[pl.ds(row, 64), lanes : lanes + 128] = (both[:, :128] / both[:, 128:]).astype(BF)
 
 
 def kernel(
@@ -69,8 +73,8 @@
     out,
     tok, we, wp, bqkv, bo, gqkv, go,
     halo_n, halo_s, halo_w, halo_e,
-    normed, normed_halo, normed_edge, expanded, acc, packed, heads_out, send1, recv1, send2, perm, unperm,
-    weight_sem, halo_send, halo_recv, send1_sem, recv1_sem, send2_sem, recv2_sem, local_sem,
+    lhs, expanded, acc, packed, heads_out, send1, recv1, send2, perm, unperm,
+    weight_sem, halo_send, halo_recv, send1_sem, recv1_sem, send2_sem, recv2_sem,
 ):
     n = lax.axis_index("ns")
     e = lax.axis_index("ew")
@@ -100,8 +104,8 @@
             [(tok_hbm, tok), (we_hbm, we), (wp_hbm, wp), (bqkv_hbm, bqkv), (bo_hbm, bo), (gqkv_hbm, gqkv), (go_hbm, go)]
         )
     ]
-    for load in loads:
-        load.start()
+    loads[0].start()
+    loads[1].start()
     pl.semaphore_wait(barrier, 37)
 
     moves = [
@@ -123,22 +127,47 @@
     for halo in halos:
         halo.start()
 
+    gain = conv_gain[...]
+
+    def expand(count, places):
+        def step(f, c):
+            cols = pl.ds(pl.multiple_of(f * 256, 256), 256)
+            hidden = gelu(dot(lhs[0:count, :], we[:, cols]))
+            at = 0
+            for r, c0, width in places:
+                for t in range(2 if r is not None else 0):
+                    expanded[2 * f + t, r, 8 + c0 : 8 + c0 + width, :] = hidden[at : at + width, 128 * t : 128 * t + 128]
+                at += width
+            return c
+
+        lax.fori_loop(0, 8, step, 0)
+
+    def stage(at, values):
+        lhs[at : at + values.shape[0], :] = values
+
+    def halo_rows(spans):
+        above = jnp.concatenate([halo_n[c0 : c0 + width, :].astype(F32) for c0, width in spans], axis=0)
+        below = jnp.concatenate([halo_s[c0 : c0 + width, :].astype(F32) for c0, width in spans], axis=0)
+        zero = jnp.zeros(above.shape, BF)
+        return jnp.concatenate(
+            [jnp.where(n > 0, layer_norm(above, gain), zero), jnp.where(n < 63, layer_norm(below, gain), zero)], axis=0
+        )
+
+    def own_rows(spans, rows):
+        x = jnp.concatenate([tok[i, c0 : c0 + width, :].astype(F32) for i in rows for c0, width in spans], axis=0)
+        return layer_norm(x, gain)
+
+    new_spans = [[(0, 24), (56, 32)], [(24, 16), (88, 16)], [(40, 16), (104, 16)], [(120, 8)]]
+
     loads[0].wait()
-    gain = conv_gain[...]
-    for i in range(8):
-        normed[i * 128 : i * 128 + 128, :] = layer_norm(tok[i].astype(F32), gain)
+    spans = new_spans[0]
+    wide = sum(width for _, width in spans)
+    for i in range(0, 8, 2):
+        stage(i * wide, own_rows(spans, (i, i + 1)))
     loads[1].wait()
-
-    def expand_own(f, c):
-        cols = pl.ds(pl.multiple_of(f * 256, 256), 256)
-        for pair in range(4):
-            hidden = gelu(dot(normed[pair * 256 : pair * 256 + 256, :], we[:, cols]))
-            for r in range(2):
-                for t in range(2):
-                    expanded[2 * f + t, 1 + pair * 2 + r, 8:136, :] = hidden[r * 128 : r * 128 + 128, 128 * t : 128 * t + 128]
-        return c
-
-    lax.fori_loop(0, 8, expand_own, 0)
+    for load in loads[2:]:
+        load.start()
+    expand(8 * wide, [(1 + i, c0, width) for i in range(8) for c0, width in spans])
 
     row = lax.broadcasted_iota(jnp.int32, (256, 256), 0)
     col = lax.broadcasted_iota(jnp.int32, (256, 256), 1)
@@ -147,9 +176,7 @@
 
     for halo in halos:
         halo.wait()
-    zero_row = jnp.zeros((128, 512), BF)
-    normed_halo[0:128, :] = jnp.where(n > 0, layer_norm(halo_n[...].astype(F32), gain), zero_row)
-    normed_halo[128:256, :] = jnp.where(n < 63, layer_norm(halo_s[...].astype(F32), gain), zero_row)
+    stage(0, halo_rows(spans))
     pick = lax.broadcasted_iota(jnp.int32, (16, 80), 1) - 8 * lax.broadcasted_iota(jnp.int32, (16, 80), 0)
     edge_row = lax.broadcasted_iota(jnp.int32, (16, 512), 0)
     rows_in = ((edge_row > 0) | (n > 0)) & ((edge_row < 9) | (n < 63))
@@ -157,26 +184,25 @@
         chosen = jnp.where(pick == at, 1.0, 0.0).astype(BF)
         tokens_edge = dot(chosen, block[...].reshape(80, 512))
         ned = layer_norm(tokens_edge, gain).astype(F32)
-        normed_edge[side * 16 : side * 16 + 16, :] = jnp.where(rows_in & there, ned, 0.0).astype(BF)
-
-    def expand_halo(f, c):
-        cols = pl.ds(pl.multiple_of(f * 256, 256), 256)
-        hidden = gelu(dot(normed_halo[...], we[:, cols]))
-        edge = gelu(dot(normed_edge[...], we[:, cols]))
-        for t in range(2):
-            lanes = slice(128 * t, 128 * t + 128)
-            expanded[2 * f + t, 0, 8:136, :] = hidden[0:128, lanes]
-            expanded[2 * f + t, 9, 8:136, :] = hidden[128:256, lanes]
-            for r in range(10):
-                expanded[2 * f + t, r, 7:8, :] = edge[r : r + 1, lanes]
-                expanded[2 * f + t, r, 136:137, :] = edge[16 + r : 17 + r, lanes]
-        return c
-
-    lax.fori_loop(0, 8, expand_halo, 0)
+        stage(2 * wide + side * 16, jnp.where(rows_in & there, ned, 0.0).astype(BF))
+    expand(
+        2 * wide + 32,
+        [(r, c0, width) for r in (0, 9) for c0, width in spans]
+        + [(r, -1, 1) for r in range(10)]
+        + [(None, None, 6)]
+        + [(r, 128, 1) for r in range(10)],
+    )
     for load in loads[2:]:
         load.wait()
 
     for quarter in range(4):
+        if quarter:
+            spans = new_spans[quarter]
+            wide = sum(width for _, width in spans)
+            for i in range(0, 8, 2):
+                stage(i * wide, own_rows(spans, (i, i + 1)))
+            stage(8 * wide, halo_rows(spans))
+            expand(10 * wide, [(r, c0, width) for r in (1, 2, 3, 4, 5, 6, 7, 8, 0, 9) for c0, width in spans])
 
         def conv(f, c, quarter=quarter):
             pieces = []
@@ -226,11 +252,10 @@
         packed[0:256, :] = dot(layer_norm(x, block_gain[...]), bqkv[...]).astype(BF)
 
         def window(w, c):
-            at = pl.multiple_of(w * 64, 64)
-            attend_window(packed, at, heads_out, at)
+            attend_windows(packed, [pl.multiple_of(w * 256 + 64 * r, 64) for r in range(4)], heads_out)
             return c
 
-        lax.fori_loop(0, 4, window, 0)
+        lax.fori_loop(0, 1, window, 0)
         acc[...] += dot(heads_out[0:256, :], bo[...])
         for j2 in range(2):
             j = 2 * quarter + j2
@@ -252,15 +277,15 @@
                     pltpu.make_async_remote_copy(
                         src_ref=send1.at[j, i],
                         dst_ref=recv1.at[half, me],
-                        send_sem=send1_sem.at[j, i],
-                        recv_sem=recv1_sem.at[half, me],
+                        send_sem=send1_sem.at[half],
+                        recv_sem=recv1_sem.at[half],
                         device_id=device(p),
                         device_id_type=MESH,
                     ).start()
 
                 @pl.when(p == me)
                 def _():
-                    pltpu.make_async_copy(send1.at[j, i], recv1.at[half, me], local_sem.at[half]).start()
+                    pltpu.make_async_copy(send1.at[j, i], recv1.at[half, me], recv1_sem.at[half]).start()
 
                 return c
 
@@ -268,20 +293,7 @@
 
     for half in range(2):
 
-        def arrive(k, c, half=half):
-            p = jnp.bitwise_xor(me, k)
-            pltpu.make_async_remote_copy(
-                src_ref=send1.at[0, 0],
-                dst_ref=recv1.at[half, p],
-                send_sem=send1_sem.at[0, 0],
-                recv_sem=recv1_sem.at[half, p],
-                device_id=device(p),
-                device_id_type=MESH,
-            ).wait_recv()
-            return c
-
-        lax.fori_loop(1, 32, arrive, 0)
-        pltpu.make_async_copy(send1.at[0, 0], recv1.at[half, me], local_sem.at[half]).wait()
+        pltpu.make_async_copy(recv1.at[half], recv1.at[half], recv1_sem.at[half]).wait()
         for u in range(2):
             x = recv1[half, 16 * u : 16 * u + 16].reshape(256, 512)
             ordered = dot(perm[...], layer_norm(x.astype(F32), grid_gain[...])).astype(BF)
@@ -290,11 +302,10 @@
                 packed[s * 64 + 32 * u : s * 64 + 32 * u + 32, :] = packed_u[s * 32 : s * 32 + 32, :]
 
         def grid_window(w, c):
-            at = pl.multiple_of(w * 64, 64)
-            attend_window(packed, at, heads_out, at)
+            attend_windows(packed, [pl.multiple_of(w * 256 + 64 * r, 64) for r in range(4)], heads_out)
             return c
 
-        lax.fori_loop(0, 8, grid_window, 0)
+        lax.fori_loop(0, 2, grid_window, 0)
         place = 32 * half + 8 * ((e % 2) * 2 + e // 2)
         for u in range(2):
             mixed = jnp.concatenate([heads_out[s * 64 + 32 * u : s * 64 + 32 * u + 32, :] for s in range(8)], axis=0)
@@ -312,47 +323,25 @@
                     pltpu.make_async_remote_copy(
                         src_ref=send2.at[half, p],
                         dst_ref=target,
-                        send_sem=send2_sem.at[half, p],
-                        recv_sem=recv2_sem.at[half, me],
+                        send_sem=send2_sem.at[half],
+                        recv_sem=recv2_sem,
                         device_id=device(p),
                         device_id_type=MESH,
                     ).start()
 
                 @pl.when(p == me)
                 def _():
-                    pltpu.make_async_copy(send2.at[half, p], target, local_sem.at[2 + half]).start()
+                    pltpu.make_async_copy(send2.at[half, p], target, recv2_sem).start()
 
                 return c
 
             lax.fori_loop(0, 16, give_back, 0)
 
-    def finish(q, c):
-        half = q // 32
-        p = q % 32
-        i = p // 4
-        strip = p % 4
-        j = 4 * half + (strip % 2) * 2 + strip // 2
-        place = 32 * half + 8 * ((strip % 2) * 2 + strip // 2)
-        target = out.at[i, :, pl.ds(pl.multiple_of(place, 8), 8), :]
-
-        @pl.when(p != me)
-        def _():
-            pltpu.make_async_remote_copy(
-                src_ref=send1.at[j, i], dst_ref=recv1.at[half, p], send_sem=send1_sem.at[j, i],
-                recv_sem=recv1_sem.at[half, p], device_id=device(p), device_id_type=MESH,
-            ).wait_send()
-            pltpu.make_async_remote_copy(
-                src_ref=send2.at[half, p], dst_ref=target, send_sem=send2_sem.at[half, p],
-                recv_sem=recv2_sem.at[half, p], device_id=device(p), device_id_type=MESH,
-            ).wait()
-
-        @pl.when(p == me)
-        def _():
-            pltpu.make_async_copy(send2.at[half, p], target, local_sem.at[2 + half]).wait()
-
-        return c
-
-    lax.fori_loop(0, 64, finish, 0)
+    for half in range(2):
+        for sem in (send1_sem, send2_sem):
+            sent = send2.at[half, 0:31]
+            pltpu.make_async_copy(sent, sent, sem.at[half]).wait()
+    pltpu.make_async_copy(out, out, recv2_sem).wait()
 
 
 def on_device(
@@ -377,9 +366,7 @@
             pltpu.VMEM((128, 512), BF),
             pltpu.VMEM((10, 8, 512), BF),
             pltpu.VMEM((10, 8, 512), BF),
-            pltpu.VMEM((1024, 512), BF),
-            pltpu.VMEM((256, 512), BF),
-            pltpu.VMEM((32, 512), BF),
+            pltpu.VMEM((448, 512), BF),
             pltpu.VMEM((16, 10, 144, 128), F32),
             pltpu.VMEM((256, 512), F32),
             pltpu.VMEM((512, 1536), BF),
@@ -392,11 +379,10 @@
             pltpu.SemaphoreType.DMA((7,)),
             pltpu.SemaphoreType.DMA((8,)),
             pltpu.SemaphoreType.DMA((8,)),
-            pltpu.SemaphoreType.DMA((8, 8)),
-            pltpu.SemaphoreType.DMA((2, 32)),
-            pltpu.SemaphoreType.DMA((2, 32)),
-            pltpu.SemaphoreType.DMA((2, 32)),
-            pltpu.SemaphoreType.DMA((4,)),
+            pltpu.SemaphoreType.DMA((2,)),
+            pltpu.SemaphoreType.DMA((2,)),
+            pltpu.SemaphoreType.DMA((2,)),
+            pltpu.SemaphoreType.DMA,
         ],
         compiler_params=pltpu.CompilerParams(
             collective_id=0, has_side_effects=True, vmem_limit_bytes=60 * 1024 * 1024

time: 84.7 us -> 82.2 us (0.970)
  Pallas kernels: 82.3 us -> 79.8 us
    pallas_call x1, Pallas kernels: 82.3 us -> 79.8 us  [on_device(): pl.pallas_call(kernel, out_shape=jax.ShapeDtypeStruct((8, 2, 64, 512), BF...]
where the time goes in v2:
time: 82.2 us; the launch traced here: 82 us
  Pallas kernels  79.8 us (97%)
  local copies, waits for them, and re-layouts  2.26 us (3%)
    pallas_call x1, Pallas kernels, on_device(): pl.pallas_call(kernel, out_shape=jax.ShapeDtypeStruct((8, 2, 64, 512), BF...  79.8 us
    unnamed x1, local copies, waits for them, and re-layouts  2.26 us

profile of v2, /device:TPU:1, one launch (start us, length us, event | category | flops | bytes accessed | tf_op | source)
XLA Modules:
  0.0 82.0 jit_solution(5173570636550434849)
XLA Ops:
  0.0 79.8 %maxvit.1 = bf16[8,2,64,512]{3,2,1,0:T(8,128)(2,1)} custom-call(bf16[8,128,512]{2,1,0:T(8,128)(2,1)} %tok_hbm.1, f32[1,512]{1,0:T(1,128)} %bitcast.5, bf16[512,2048]{1,0:T(8,128)(2,1)} %we_hbm.1, f32[3,3,2048]{2,1,0:T(4,128)} %dw.1, bf16[2048,512]{1,0:T(8,128)(2,1)} %wp_hbm.1, f32[1,512]{1,0:T(1,128)} %bitcast.6, bf16[512,1536]{1,0:T(8,128)(2,1)} %bqkv_hbm.1, ...), custom_call_target="tpu_custom_call" | custom-call | tf_op jit(solution)/shard_map/maxvit/pallas_call | solution.py:352
  79.8 2.3 %copy.13 = bf16[8,128,512]{2,1,0:T(8,128)(2,1)} copy(bf16[8,128,512]{2,1,0:T(8,128)(2,1)} %bitcast.4) | data formatting | bytes 2097152
